TPU v7x, 32 devices: a whole 2x2x4 slice. The times are simulated.
32 devices in a mesh: sym: 4 (over y, core), slab: 8 (over z, x).
Axes of the slice: x: 2, y: 2, z: 4, core: 2. Of those that a mesh axis runs over, the one named last changes fastest.
Arguments:
- coefficients: float32 [8, 8192, 128], P('sym', 'slab'), may hold values from -6 to 6
- dipole: bfloat16 [8, 8192, 8192], P('sym', 'slab'), may hold values from -0.09375 to 0.09375
- energies: float32 [8, 8192], P('sym', 'slab'), may hold values from -3 to 3
- pulse_field: float32 [64], replicated, may hold values from 0.5 to 2
- live_states: int32 [8], replicated, may hold values from 4096 to 8192, as said below
Outputs:
- adjoint: float32 [8, 8192, 128], P('sym', 'slab')
Inputs may be any that keep to these rules, and one draw needn't show every extreme that they name: live_states[L] counts the states in use in symmetry block L; positions at or beyond it are padding; some block uses all 8192.
All inputs are finite; a program needn't handle non-finite values.
Results may differ from a plain program's by a relative error of at most 0.0012.
Values may be sent and summed in bfloat16 or wider, within the bound.
A program may use at most 128 MiB of HBM per device.

v0:
```python
import jax
import jax.numpy as jnp
from jax import lax
from jax.sharding import PartitionSpec as P

step_size = 0.2


def from_behind(value, axis, steps):
    count = lax.axis_size(axis)
    initial, last = (max(0, -steps), min(count, count - steps))
    return lax.ppermute(value, axis, [(source, source + steps) for source in range(initial, last)])


def rotate(values):
    half = values.shape[-1] // 2
    return jnp.concatenate([-values[..., half:], values[..., :half]], axis=-1)


def local(coefficients, dipole, energies, pulse_field, live_states):
    n_local, n_rows, n_cols = coefficients.shape
    n_sym = n_local * lax.axis_size("sym")
    first_block = lax.axis_index("sym") * n_local
    block_ids = first_block + jnp.arange(n_local, dtype=jnp.int32)
    live_here = lax.dynamic_slice_in_dim(live_states, first_block, n_local)
    upper_on = (block_ids < n_sym - 1).astype(jnp.float32)
    row_ids = lax.axis_index("slab") * n_rows + jnp.arange(n_rows, dtype=jnp.int32)
    live_mask = (row_ids[None, :] < live_here[:, None]).astype(jnp.float32)
    column_gain = jnp.concatenate([pulse_field, pulse_field])

    def hamiltonian(amplitude):
        amplitude_bf = amplitude.astype(jnp.bfloat16)
        next_rows = from_behind(amplitude_bf[0], "sym", -1)
        upper_rows = jnp.concatenate([amplitude_bf[1:], next_rows[None]], axis=0)
        row_panel = dipole
        forward = jnp.einsum(
            "srk,skc->src",
            row_panel,
            lax.all_gather(upper_rows, "slab", axis=1, tiled=True),
            preferred_element_type=jnp.float32,
        )
        row_panel = dipole
        summed = lax.psum_scatter(
            jnp.einsum("srk,src->ksc", row_panel, amplitude_bf, preferred_element_type=jnp.float32),
            "slab",
            scatter_dimension=0,
            tiled=True,
        )
        backward = jnp.transpose(summed, (1, 0, 2))
        forward = forward * upper_on[:, None, None]
        backward = backward * upper_on[:, None, None]
        from_below = from_behind(backward[n_local - 1], "sym", 1)
        lowered = jnp.concatenate([from_below[None], backward[: n_local - 1]], axis=0)
        return live_mask[:, :, None] * (
            energies[:, :, None] * amplitude + column_gain * (forward + lowered)
        )

    start_state = live_mask[:, :, None] * coefficients
    first_term = step_size * rotate(hamiltonian(start_state))
    second_term = 0.5 * step_size * rotate(hamiltonian(first_term))
    return start_state + first_term + second_term


def solution(mesh):
    placed = (P("sym", "slab", None), P("sym", "slab", None), P("sym", "slab"), P(), P())
    return jax.shard_map(
        local, mesh=mesh, in_specs=placed, out_specs=P("sym", "slab", None), check_vma=False
    )
```

profile of v0, /device:TPU:0, one launch (start us, length us, event | category | flops | bytes accessed | tf_op | source)
XLA Modules:
  0.0 538.5 jit_solution(6066322774966613044)
XLA Ops:
  6.5 1.6 copy.6
  8.1 0.7 dynamic_slice.3
  8.8 0.1 compare_convert_fusion
  8.9 0.1 multiply_convert_fusion.1
  9.0 18.3 %convolution_bitcast_fusion.1 = f32[8192,2,128]{0,2,1:T(8,128)} fusion(bf16[2,1024,128]{1,2,0:T(8,128)(2,1)S(1)} %multiply_convert_fusion.1, bf16[2,1024,8192]{2,1,0:T(8,128)(2,1)} %param.6), kind=kOutput, calls=%fused_computation.1 | convolution fusion | flops 4294967296 | bytes 42467328 | tf_op jit(solution)/shard_map/srk,src->ksc/dot_general | solution.py:44
  27.5 1.3 collective-permute-start
  28.8 2.1 collective-permute-done
  30.9 0.8 pad_maximum_fusion.1
  31.8 0.0 reduce-scatter.5.cloned.1.call-start
  31.8 147.8 %reduce-scatter.3.cloned.1.call-done = f32[1024,2,128]{0,2,1:T(8,128)} async-done(((f32[8192,2,128]{0,2,1:T(8,128)}), f32[1024,2,128]{0,2,1:T(8,128)}) %reduce-scatter.3.cloned.1.call-update) | async-done | bytes 1048592 | tf_op jit(solution)/shard_map/reduce_scatter | solution.py:43
  179.6 1.4 multiply_bitcast_fusion.1
  181.0 0.1 slice_bitcast_fusion.1
  181.1 2.0 collective-permute-start.1
  183.1 0.1 pad_maximum_fusion.3
  183.2 71.2 %all-gather.3.cloned.1.call-done = bf16[2,8192,128]{1,2,0:T(8,128)(2,1)} async-done(((bf16[2,1024,128]{1,2,0:T(8,128)(2,1)}), bf16[2,8192,128]{1,2,0:T(8,128)(2,1)}) %all-gather.3.cloned.1.call-update) | async-done | bytes 4194320 | tf_op jit(solution)/shard_map/all_gather | solution.py:39
  254.5 17.0 %fusion.5 = f32[2,1024,128]{1,2,0:T(8,128)S(1)} fusion(bf16[2,8192,128]{1,2,0:T(8,128)(2,1)} %all-gather.3.cloned.1.call-done, bf16[2,1024,8192]{2,1,0:T(8,128)(2,1)} %param.6, f32[1,1024,128]{1,2,0:T(8,128)S(1)} %get-tuple-element.12, f32[1,1024,128]{1,2,0:T(8,128)S(1)} %bitcast.49, f32[2,1024,128]{1,2,0:T(8,128)S(1)} %copy.6, ...), kind=kOutput, calls=%fused_computation.9 | convolution fusion | flops 4297064448 | bytes 40911368 | tf_op jit(solution)/shard_map/srk,skc->src/dot_general | solution.py:36
  271.5 0.1 slice_negate_fusion.1
  271.6 0.1 multiply_convert_fusion
  271.7 18.3 %convolution_bitcast_fusion = f32[8192,2,128]{0,2,1:T(8,128)} fusion(bf16[2,1024,128]{1,2,0:T(8,128)(2,1)S(1)} %multiply_convert_fusion, bf16[2,1024,8192]{2,1,0:T(8,128)(2,1)} %param.6), kind=kOutput, calls=%fused_computation | convolution fusion | flops 4294967296 | bytes 42467328 | tf_op jit(solution)/shard_map/srk,src->ksc/dot_general | solution.py:44
  290.1 1.3 collective-permute-start.2
  291.4 2.1 collective-permute-done.2
  293.6 0.8 pad_maximum_fusion.2
  294.4 143.4 %reduce-scatter.5.cloned.1.call-done = f32[1024,2,128]{0,2,1:T(8,128)} async-done(((f32[8192,2,128]{0,2,1:T(8,128)}), f32[1024,2,128]{0,2,1:T(8,128)}) %reduce-scatter.5.cloned.1.call-update) | async-done | bytes 1048592 | tf_op jit(solution)/shard_map/reduce_scatter | solution.py:43
  437.9 1.4 multiply_bitcast_fusion
  439.3 0.9 slice_bitcast_fusion
  440.2 1.8 collective-permute-start.3
  442.0 70.3 %all-gather.5.cloned.1.call-done = bf16[2,8192,128]{1,2,0:T(8,128)(2,1)} async-done(((bf16[2,1024,128]{1,2,0:T(8,128)(2,1)}), bf16[2,8192,128]{1,2,0:T(8,128)(2,1)}) %all-gather.5.cloned.1.call-update) | async-done | bytes 4194320 | tf_op jit(solution)/shard_map/all_gather | solution.py:39
  512.3 0.8 copy-done
  513.1 17.1 %fusion.9 = f32[2,1024,128]{1,2,0:T(8,128)S(1)} fusion(bf16[2,8192,128]{1,2,0:T(8,128)(2,1)} %all-gather.5.cloned.1.call-done, bf16[2,1024,8192]{2,1,0:T(8,128)(2,1)} %param.6, f32[1,1024,128]{1,2,0:T(8,128)} %get-tuple-element.8, f32[1,1024,128]{1,2,0:T(8,128)} %bitcast.48, f32[2,1024,64]{1,2,0:T(8,128)S(1)} %get-tuple-element.10, ...), kind=kOutput, calls=%fused_computation.13 | convolution fusion | flops 4297064448 | bytes 40911368 | tf_op jit(solution)/shard_map/srk,skc->src/dot_general | solution.py:36
  530.3 0.1 slice_negate_fusion
  530.4 0.3 fusion.10
  530.7 1.3 copy.7
  (19 shorter events, 0.3 us)
Async XLA Ops:
  6.5 173.1 %reduce-scatter.3.cloned.1.call-start = ((), (), s32[]{:S(2)}) async-start(), calls=%async_computation.3 | async-start | bytes 9437184 | tf_op jit(solution)/shard_map/reduce_scatter | solution.py:43
  9.0 174.1 %copy-start.2 = (f32[64]{0:T(128)S(1)}, f32[64]{0:T(128)}, u32[]{:S(2)}) copy-start(f32[64]{0:T(128)} %param.8) | copy-start | bytes 772
  9.0 245.4 %copy-start.1 = (f32[2,1024]{1,0:T(2,128)S(1)}, f32[2,1024]{1,0:T(2,128)}, u32[]{:S(2)}) copy-start(f32[2,1024]{1,0:T(2,128)} %param.7) | copy-start | bytes 24580
  27.4 227.1 %all-gather.3.cloned.1.call-start = ((), (), s32[]{:S(2)}) async-start(), calls=%async_computation.2 | async-start | bytes 4718592 | tf_op jit(solution)/shard_map/all_gather | solution.py:39
  27.5 3.4 collective-permute-start
  31.8 406.1 %reduce-scatter.5.cloned.1.call-start = ((), (), s32[]{:S(2)}) async-start(), calls=%async_computation.5 | async-start | bytes 9437184 | tf_op jit(solution)/shard_map/reduce_scatter | solution.py:43
  181.1 73.3 %collective-permute-start.1 = (f32[1024,128]{0,1:T(8,128)S(1)}, f32[1024,128]{0,1:T(8,128)S(1)}, u32[]{:S(2)}, u32[]{:S(2)}) collective-permute-start(f32[1024,128]{0,1:T(8,128)S(1)} %get-tuple-element.11), channel_id=1, source_target_pairs={{0,8},{8,16},{16,24},{1,9},{9,17},{17,25},{2,10},{10,18},{18,26},{... | collective-permute-start | bytes 1572872 | tf_op jit(solution)/shard_map/ppermute | solution.py:12
  290.1 222.3 %all-gather.5.cloned.1.call-start = ((), (), s32[]{:S(2)}) async-start(), calls=%async_computation.4 | async-start | bytes 4718592 | tf_op jit(solution)/shard_map/all_gather | solution.py:39
  290.1 3.4 collective-permute-start.2
  440.2 72.2 %collective-permute-start.3 = (f32[1024,128]{0,1:T(8,128)S(1)}, f32[1024,128]{0,1:T(8,128)S(1)}, u32[]{:S(2)}, u32[]{:S(2)}) collective-permute-start(f32[1024,128]{0,1:T(8,128)S(1)} %get-tuple-element.7), channel_id=1, source_target_pairs={{0,8},{8,16},{16,24},{1,9},{9,17},{17,25},{2,10},{10,18},{18,26},{... | collective-permute-start | bytes 1572872 | tf_op jit(solution)/shard_map/ppermute | solution.py:12
  512.3 0.8 copy-start
Sparse Core Ops, SparseCore 0:
  27.5 152.0 reduce-scatter.2
  182.0 72.3 all-gather.2
  290.2 147.6 reduce-scatter.4
  439.9 72.3 all-gather.4
where the time goes:
time: 539 us
  waiting for transfers between devices  437 us (81%)
  matrix products  70.8 us (13%)
  between operations  13.3 us (2%)
  starting transfers between devices  6.53 us (1%)
  local copies, waits for them, and re-layouts  5.44 us (1%)
    reduce_scatter x2, waiting for transfers between devices, hamiltonian(): lax.psum_scatter(jnp.einsum('srk,src->ksc', row_panel, amplitude_bf, pref...  291 us
    all_gather x2, waiting for transfers between devices, hamiltonian(): lax.all_gather(upper_rows, 'slab', axis=1, tiled=True)  142 us
    dot_general x2, matrix products, hamiltonian(): jnp.einsum('srk,src->ksc', row_panel, amplitude_bf, preferred_element_typ...  36.7 us
    dot_general x2, matrix products, hamiltonian(): jnp.einsum('srk,skc->src', row_panel, lax.all_gather(upper_rows, 'slab',...  34.2 us
  transfers between devices with their start and end apart: 8, of which 6 were waited for; matrix products, arithmetic and copies ran while one was open for 1% of the time, Pallas kernels for 0%

commit v1 on v0

v1 whole, which is shorter than its diff:
```python
import functools

import jax
import jax.numpy as jnp
from jax import lax
from jax.experimental import pallas as pl
from jax.experimental.pallas import tpu as pltpu
from jax.sharding import PartitionSpec as P

step_size = 0.2
MESH = pl.DeviceIdType.MESH


def kernel(
    n, n_sym_dev, start_ref, dip_ref, energy_ref, mask_ref, gain_ref, out_ref,
    dip, gath, rs_send, rs_recv, u_rows, u_cols, acc, state, low, low_send, low_recv,
    load_sem, start_sem, ag_send_sem, ag_recv_sem, rs_send_sem, rs_recv_sem, sym_send_sem, sym_recv_sem,
):
    n_local, cols, rows = out_ref.shape
    width = dip.shape[-1]
    half = n // 2
    last = n_local - 1
    side = rows // 2
    mid = cols // 2
    s = lax.axis_index("sym")
    me = lax.axis_index("slab")
    odd = me % 2
    pos = (1 - odd) * (me // 2) + odd * (n - 1 - me // 2)

    def at(offset):
        place = (pos + offset + n) % n
        back = place // half
        return (1 - back) * (2 * place) + back * (2 * (n - place) - 1)

    ring = (at(1), at(-1))
    sym_up = (s + 1) % n_sym_dev
    sym_down = (s + n_sym_dev - 1) % n_sym_dev
    sign = (1, -1)

    barrier = pltpu.get_barrier_semaphore()
    for peer in ((s, ring[0]), (s, ring[1]), (sym_up, me), (sym_down, me)):
        pl.semaphore_signal(barrier, inc=1, device_id=peer, device_id_type=MESH)

    def load(b, d):
        j = at(half + d)
        return pltpu.make_async_copy(
            dip_ref.at[b, :, pl.ds(pl.multiple_of(j * width, width), width)],
            dip.at[b, j],
            load_sem.at[b, d],
        )

    first_state = pltpu.make_async_copy(start_ref, state, start_sem)
    first_state.start()
    for b in reversed(range(n_local)):
        load(b, 0).start()

    def start_rest(d, carry):
        for b in range(n_local):
            load(b, d).start()
        return carry

    def wait_rest(d, carry):
        for b in range(n_local):
            load(b, d).wait()
        return carry

    lax.fori_loop(1, n, start_rest, 0)
    first_state.wait()
    out_ref[...] = state[...]
    pl.semaphore_wait(barrier, 4)

    def step(h, carry):
        def ag_copy(b, g, k, owner):
            slot = gath.at[h, b, owner]
            if k == half - 1:
                slot = gath.at[h, b, owner, pl.ds(g * side, side)]
            return pltpu.make_async_remote_copy(
                src_ref=slot, dst_ref=slot,
                send_sem=ag_send_sem.at[h, b, g, k], recv_sem=ag_recv_sem.at[h, b, g, k],
                device_id=(s, ring[g]), device_id_type=MESH,
            )

        def ag_out(b, g, k):
            return ag_copy(b, g, k, at(-sign[g] * k))

        def ag_in(b, g, k):
            return ag_copy(b, g, k, at(-sign[g] * (k + 1)))

        def rs_copy(b, g, k):
            source, target = rs_send.at[b, g, k], rs_recv.at[h, b, g, k]
            if k == 0:
                piece = pl.ds(g * mid, mid)
                source, target = rs_send.at[b, g, k, piece], rs_recv.at[h, b, g, k, piece]
            return pltpu.make_async_remote_copy(
                src_ref=source, dst_ref=target,
                send_sem=rs_send_sem.at[h, b, g, k], recv_sem=rs_recv_sem.at[h, b, g, k],
                device_id=(s, ring[g]), device_id_type=MESH,
            )

        def sym_rows():
            return pltpu.make_async_remote_copy(
                src_ref=u_rows, dst_ref=gath.at[h, last, me],
                send_sem=sym_send_sem.at[h, 0], recv_sem=sym_recv_sem.at[h, 0],
                device_id=(sym_down, me), device_id_type=MESH,
            )

        def sym_low():
            return pltpu.make_async_remote_copy(
                src_ref=low_send, dst_ref=low_recv.at[h],
                send_sem=sym_send_sem.at[h, 1], recv_sem=sym_recv_sem.at[h, 1],
                device_id=(sym_up, me), device_id_type=MESH,
            )

        tile = min(256, width)

        def over_tiles(b, j, emit):
            def one(t, c):
                piece = pl.ds(pl.multiple_of(t * tile, tile), tile)
                emit(piece, jnp.dot(u_cols[b], dip[b, j, :, piece], preferred_element_type=jnp.float32))
                return c

            lax.fori_loop(0, width // tile, one, 0)

        def rs_first(b):
            def emit(piece, value):
                value = value.astype(jnp.bfloat16)
                rs_send[b, 0, 0, :mid, piece] = value[:mid]
                rs_send[b, 1, 0, mid:, piece] = value[mid:]

            over_tiles(b, at(half), emit)
            for g in range(2):
                rs_copy(b, g, 0).start()

        def add_hop(b, g, k, piece, value):
            if k == 0:
                got = rs_recv[h, b, g, 0, g * mid:(g + 1) * mid, piece].astype(jnp.float32)
                parts = [value[:mid], value[mid:]]
                parts[g] = parts[g] + got
                return jnp.concatenate(parts, axis=0)
            return value + rs_recv[h, b, g, k, :, piece].astype(jnp.float32)

        def rs_hop(b, g, k):
            rs_copy(b, g, k - 1).wait_recv()

            def emit(piece, value):
                rs_send[b, g, k, :, piece] = add_hop(b, g, k - 1, piece, value).astype(jnp.bfloat16)

            over_tiles(b, at(sign[g] * (half - k)), emit)
            rs_copy(b, g, k).start()

        def rs_last(b, target):
            for g in range(2):
                rs_copy(b, g, half - 1).wait_recv()

            def emit(piece, value):
                for g in range(2):
                    value = add_hop(b, g, half - 1, piece, value)
                target[:, piece] = value

            over_tiles(b, me, emit)

        row_tile = min(256, rows)

        def forward(b, j, first=False):
            def one(t, c):
                piece = pl.ds(pl.multiple_of(t * row_tile, row_tile), row_tile)
                value = jnp.dot(dip[b, j, piece, :], gath[h, b, j], preferred_element_type=jnp.float32)
                acc[b, piece, :] = value if first else acc[b, piece, :] + value
                return c

            lax.fori_loop(0, rows // row_tile, one, 0)

        u_rows[...] = state[0].T.astype(jnp.bfloat16)
        sym_rows().start()
        for b in range(last):
            gath[h, b, me] = state[b + 1].T.astype(jnp.bfloat16)
            for g in range(2):
                ag_out(b, g, 0).start()
        for b in range(n_local):
            u_cols[b] = state[b].astype(jnp.bfloat16)

        for b in reversed(range(n_local)):
            @pl.when(h == 0)
            def _():
                load(b, 0).wait()

            rs_first(b)
            if b == last:
                sym_rows().wait_recv()
                for g in range(2):
                    ag_out(last, g, 0).start()

        @pl.when(h == 0)
        def _():
            lax.fori_loop(1, n, wait_rest, 0)

        for b in range(n_local):
            forward(b, me, first=True)

        for k in range(1, half):
            for b in range(n_local):
                for g in range(2):
                    ag_in(b, g, k - 1).wait_recv()
                    ag_out(b, g, k).start()
                for g in range(2):
                    rs_hop(last - b, g, k)
            for b in range(n_local):
                for g in range(2):
                    forward(b, at(-sign[g] * k))

        rs_last(last, low_send)
        sym_low().start()
        for b in range(last):
            rs_last(b, low.at[b])
        for b in range(n_local):
            for g in range(2):
                ag_in(b, g, half - 1).wait_recv()
            forward(b, at(half))

        sym_low().wait_recv()
        scale = step_size / (h + 1).astype(jnp.float32)
        for b in range(n_local):
            upper = acc[b].T
            if b == 0:
                lower = low_recv[h] * (s > 0).astype(jnp.float32)
            else:
                lower = low[b - 1]
            if b == last:
                upper = upper * (s < n_sym_dev - 1).astype(jnp.float32)
            applied = mask_ref[b] * (energy_ref[b] * state[b] + gain_ref[...] * (upper + lower))
            turned = scale * jnp.concatenate([-applied[mid:], applied[:mid]], axis=0)
            state[b] = turned
            out_ref[b] = out_ref[b] + turned

        sym_rows().wait_send()
        sym_low().wait_send()
        for b in range(n_local):
            for g in range(2):
                for k in range(half):
                    ag_out(b, g, k).wait_send()
                    rs_copy(b, g, k).wait_send()
        return carry

    lax.fori_loop(0, 2, step, 0)


def local(coefficients, dipole, energies, pulse_field, live_states):
    n_local, n_rows, n_cols = coefficients.shape
    n = lax.axis_size("slab")
    n_sym_dev = lax.axis_size("sym")
    width = dipole.shape[2] // n
    first_block = lax.axis_index("sym") * n_local
    live_here = lax.dynamic_slice_in_dim(live_states, first_block, n_local)
    row_ids = lax.axis_index("slab") * n_rows + jnp.arange(n_rows, dtype=jnp.int32)
    live_mask = (row_ids[None, :] < live_here[:, None]).astype(jnp.float32)[:, None, :]
    column_gain = jnp.concatenate([pulse_field, pulse_field])[:, None]
    start_state = live_mask * jnp.transpose(coefficients, (0, 2, 1))
    half = n // 2
    hops = (2, n_local, 2, half)
    f32, bf16 = jnp.float32, jnp.bfloat16
    vmem = pl.BlockSpec(memory_space=pltpu.VMEM)
    hbm = pl.BlockSpec(memory_space=pl.ANY)
    dma = pltpu.SemaphoreType.DMA
    flops = 8 * n_local * n_rows * dipole.shape[2] * n_cols
    adjoint = pl.pallas_call(
        functools.partial(kernel, n, n_sym_dev),
        out_shape=jax.ShapeDtypeStruct((n_local, n_cols, n_rows), f32),
        in_specs=[hbm, hbm, vmem, vmem, vmem],
        out_specs=vmem,
        scratch_shapes=[
            pltpu.VMEM((n_local, n, n_rows, width), bf16),
            pltpu.VMEM((2, n_local, n, n_rows, n_cols), bf16),
            pltpu.VMEM((n_local, 2, half, n_cols, n_rows), bf16),
            pltpu.VMEM((2, n_local, 2, half, n_cols, n_rows), bf16),
            pltpu.VMEM((n_rows, n_cols), bf16),
            pltpu.VMEM((n_local, n_cols, n_rows), bf16),
            pltpu.VMEM((n_local, n_rows, n_cols), f32),
            pltpu.VMEM((n_local, n_cols, n_rows), f32),
            pltpu.VMEM((max(1, n_local - 1), n_cols, n_rows), f32),
            pltpu.VMEM((n_cols, n_rows), f32),
            pltpu.VMEM((2, n_cols, n_rows), f32),
            dma((n_local, n)),
            dma,
            dma(hops), dma(hops), dma(hops), dma(hops),
            dma((2, 2)), dma((2, 2)),
        ],
        compiler_params=pltpu.CompilerParams(
            collective_id=0, has_side_effects=True, vmem_limit_bytes=62 * 2**20
        ),
        cost_estimate=pl.CostEstimate(flops=flops, bytes_accessed=2 * dipole.size, transcendentals=0),
    )(start_state, dipole, energies[:, None, :], live_mask, column_gain)
    return jnp.transpose(adjoint, (0, 2, 1))


def solution(mesh):
    placed = (P("sym", "slab", None), P("sym", "slab", None), P("sym", "slab"), P(), P())
    return jax.shard_map(
        local, mesh=mesh, in_specs=placed, out_specs=P("sym", "slab", None), check_vma=False
    )
```

time: 539 us -> 186 us (0.35)
  waiting for transfers between devices: 437 us -> 0 us
  Pallas kernels: 0 us -> 177 us
  matrix products: 70.8 us -> 0 us
  between operations: 13.3 us -> 0.02 us
  starting transfers between devices: 6.53 us -> 0 us
    reduce_scatter x2 -> x0, waiting for transfers between devices: 291 us -> none  [hamiltonian(): lax.psum_scatter(jnp.einsum('srk,src->ksc', row_panel, amplitude_bf, pref...]
    pallas_call x0 -> x1, Pallas kernels: none -> 177 us  [local(): pl.pallas_call(functools.partial(kernel, n, n_sym_dev), out_shape=jax.Sha...]
    all_gather x2 -> x0, waiting for transfers between devices: 142 us -> none  [hamiltonian(): lax.all_gather(upper_rows, 'slab', axis=1, tiled=True)]
    dot_general x4 -> x0, matrix products: 70.8 us -> none  [the longest x2 36.7 us: hamiltonian(): jnp.einsum('srk,src->ksc', row_panel, amplitude_bf, preferred_element_typ...]
    ppermute x4 -> x0, starting transfers between devices: 6.4 us -> none  [from_behind(): lax.ppermute(value, axis, [(source, source + steps) for source in range(i...]
  transfers between devices with their start and end apart: 8 -> 0, of which waited for: 6 -> 0; matrix products, arithmetic and copies ran while one was open for 1% -> 0% of each run, Pallas kernels for 0% -> 0%
where the time goes in v1:
time: 186 us
  Pallas kernels  177 us (95%)
  local copies, waits for them, and re-layouts  6.85 us (4%)
  other arithmetic  2.64 us (1%)
    pallas_call x1, Pallas kernels, local(): pl.pallas_call(functools.partial(kernel, n, n_sym_dev), out_shape=jax.Sha...  177 us

profile of v1, /device:TPU:0, one launch (start us, length us, event | category | flops | bytes accessed | tf_op | source)
XLA Modules:
  0.0 186.1 jit_solution(12014361345801432080)
XLA Ops:
  0.0 0.7 dynamic_slice.3
  0.7 0.8 maximum_bitcast_fusion
  1.5 0.7 compare_convert_fusion.mask_ref
  2.2 0.1 compare_convert_fusion.1
  2.3 1.3 broadcast_in_dim.4.energy_ref
  3.6 0.7 copy.7.gain_ref
  4.3 1.6 copy.6
  5.9 1.1 multiply_bitcast_fusion.start_ref
  7.0 176.6 %shard_map.55 = f32[2,128,1024]{2,1,0:T(8,128)} custom-call(f32[2,128,1024]{2,1,0:T(8,128)} %multiply_bitcast_fusion.start_ref, bf16[2,1024,8192]{2,1,0:T(8,128)(2,1)} %dip_ref.1, f32[2,1,1024]{2,1,0:T(1,128)} %broadcast_in_dim.4.energy_ref, f32[2,1,1024]{2,1,0:T(1,128)} %compare_convert_fusion.mask_ref, f32[128,1]{1,0:T(8,128)} %copy.7.gain_ref), custom_call_target="tpu_custom_call" | custom-call | flops 17179869184 | bytes 33554432 | tf_op jit(solution)/shard_map/pallas_call | solution.py:265
  183.6 2.5 %copy.8 = f32[2,1024,128]{2,1,0:T(8,128)} copy(f32[2,1024,128]{1,2,0:T(8,128)} %bitcast.5) | data formatting | bytes 2097152 | tf_op jit(solution)/shard_map/transpose | solution.py:292
  (1 shorter events, 0.0 us)

commit v2 on v0

v2 whole, which is shorter than its diff:
```python
import functools

import jax
import jax.numpy as jnp
from jax import lax
from jax.experimental import pallas as pl
from jax.experimental.pallas import tpu as pltpu
from jax.sharding import PartitionSpec as P

step_size = 0.2
MESH = pl.DeviceIdType.MESH


def kernel(
    n, n_sym_dev, start_ref, dip_ref, energy_ref, mask_ref, gain_ref, out_ref,
    dip, gath, rs_send, rs_recv, u_rows, u_cols, acc, state, low, low_send, low_recv,
    load_sem, start_sem, ag_send_sem, ag_recv_sem, rs_send_sem, rs_recv_sem, sym_send_sem, sym_recv_sem,
):
    n_local, cols, rows = out_ref.shape
    width = dip.shape[-1]
    half = n // 2
    side = rows // 2
    mid = cols // 2
    s = lax.axis_index("sym")
    me = lax.axis_index("slab")
    odd = me % 2
    pos = (1 - odd) * (me // 2) + odd * (n - 1 - me // 2)

    def at(offset):
        place = (pos + offset + n) % n
        back = place // half
        return (1 - back) * (2 * place) + back * (2 * (n - place) - 1)

    ring = (at(1), at(-1))
    sym_up = (s + 1) % n_sym_dev
    sym_down = (s + n_sym_dev - 1) % n_sym_dev
    sign = (1, -1)

    barrier = pltpu.get_barrier_semaphore()
    for peer in ((s, ring[0]), (s, ring[1]), (sym_up, me), (sym_down, me)):
        pl.semaphore_signal(barrier, inc=1, device_id=peer, device_id_type=MESH)

    def load(b, d):
        j = at(half + d)
        return pltpu.make_async_copy(
            dip_ref.at[b, :, pl.ds(pl.multiple_of(j * width, width), width)],
            dip.at[b, j],
            load_sem.at[b, d],
        )

    def start_load(b):
        def one(d, carry):
            load(b, d).start()
            return carry

        return one

    def wait_load(b):
        def one(d, carry):
            load(b, d).wait()
            return carry

        return one

    first_state = pltpu.make_async_copy(start_ref, state, start_sem)
    first_state.start()
    lax.fori_loop(0, n, start_load(0), 0)
    lax.fori_loop(0, n, start_load(1), 0)
    first_state.wait()

    def ag_copy(h, b, g, k, owner):
        slot = gath.at[h, b, owner]
        if k == half - 1:
            slot = gath.at[h, b, owner, pl.ds(g * side, side)]
        return pltpu.make_async_remote_copy(
            src_ref=slot, dst_ref=slot,
            send_sem=ag_send_sem.at[h, b, g, k], recv_sem=ag_recv_sem.at[h, b, g, k],
            device_id=(s, ring[g]), device_id_type=MESH,
        )

    def ag_out(h, b, g, k):
        return ag_copy(h, b, g, k, at(-sign[g] * k))

    def ag_in(h, b, g, k):
        return ag_copy(h, b, g, k, at(-sign[g] * (k + 1)))

    def rs_copy(h, b, g, k):
        source, target = rs_send.at[b, g, k], rs_recv.at[h, b, g, k]
        if k == 0:
            piece = pl.ds(g * mid, mid)
            source, target = rs_send.at[b, g, k, piece], rs_recv.at[h, b, g, k, piece]
        return pltpu.make_async_remote_copy(
            src_ref=source, dst_ref=target,
            send_sem=rs_send_sem.at[h, b, g, k], recv_sem=rs_recv_sem.at[h, b, g, k],
            device_id=(s, ring[g]), device_id_type=MESH,
        )

    def sym_rows(h):
        return pltpu.make_async_remote_copy(
            src_ref=u_rows, dst_ref=gath.at[h, 1, me],
            send_sem=sym_send_sem.at[h, 0], recv_sem=sym_recv_sem.at[h, 0],
            device_id=(sym_down, me), device_id_type=MESH,
        )

    def sym_low(h):
        return pltpu.make_async_remote_copy(
            src_ref=low_send, dst_ref=low_recv.at[h],
            send_sem=sym_send_sem.at[h, 1], recv_sem=sym_recv_sem.at[h, 1],
            device_id=(sym_up, me), device_id_type=MESH,
        )

    tile = min(256, width)
    row_tile = min(256, rows)

    def over_tiles(h, b, j, emit):
        def one(t, c):
            piece = pl.ds(pl.multiple_of(t * tile, tile), tile)
            emit(piece, jnp.dot(u_cols[h, b], dip[b, j, :, piece], preferred_element_type=jnp.float32))
            return c

        lax.fori_loop(0, width // tile, one, 0)

    def add_hop(h, b, g, k, piece, value):
        if k == 0:
            got = rs_recv[h, b, g, 0, g * mid:(g + 1) * mid, piece].astype(jnp.float32)
            parts = [value[:mid], value[mid:]]
            parts[g] = parts[g] + got
            return jnp.concatenate(parts, axis=0)
        return value + rs_recv[h, b, g, k, :, piece].astype(jnp.float32)

    def rs_free(h, b, g, k):
        if h == 1:
            rs_copy(0, b, g, k).wait_send()

    def rs_first(h, b):
        def emit(piece, value):
            value = value.astype(jnp.bfloat16)
            rs_send[b, 0, 0, :mid, piece] = value[:mid]
            rs_send[b, 1, 0, mid:, piece] = value[mid:]

        for g in range(2):
            rs_free(h, b, g, 0)
        over_tiles(h, b, at(half), emit)
        for g in range(2):
            rs_copy(h, b, g, 0).start()

    def rs_hop(h, b, g, k):
        rs_free(h, b, g, k)
        rs_copy(h, b, g, k - 1).wait_recv()

        def emit(piece, value):
            rs_send[b, g, k, :, piece] = add_hop(h, b, g, k - 1, piece, value).astype(jnp.bfloat16)

        over_tiles(h, b, at(sign[g] * (half - k)), emit)
        rs_copy(h, b, g, k).start()

    def rs_last(h, b, target):
        for g in range(2):
            rs_copy(h, b, g, half - 1).wait_recv()

        def emit(piece, value):
            for g in range(2):
                value = add_hop(h, b, g, half - 1, piece, value)
            target[:, piece] = value

        over_tiles(h, b, me, emit)

    def forward(h, b, j, first=False):
        def one(t, c):
            piece = pl.ds(pl.multiple_of(t * row_tile, row_tile), row_tile)
            value = jnp.dot(dip[b, j, piece, :], gath[h, b, j], preferred_element_type=jnp.float32)
            acc[h, b, piece, :] = value if first else acc[h, b, piece, :] + value
            return c

        lax.fori_loop(0, rows // row_tile, one, 0)

    def present(h, b):
        if b == 0:
            if h == 1:
                sym_rows(0).wait_send()
            u_rows[...] = state[0].T.astype(jnp.bfloat16)
            sym_rows(h).start()
        else:
            gath[h, 0, me] = state[1].T.astype(jnp.bfloat16)
        u_cols[h, b] = state[b].astype(jnp.bfloat16)

    def begin(h, c):
        if c == 0:
            for g in range(2):
                ag_out(h, 0, g, 0).start()
        rs_first(h, 1 - c)
        if c == 1:
            sym_rows(h).wait_recv()
            for g in range(2):
                ag_out(h, 1, g, 0).start()

    def finish(h, c):
        upper = acc[h, c].T
        if c == 0:
            sym_low(h).wait_recv()
            lower = low_recv[h] * (s > 0).astype(jnp.float32)
        else:
            lower = low[...]
            upper = upper * (s < n_sym_dev - 1).astype(jnp.float32)
        applied = mask_ref[c] * (energy_ref[c] * state[c] + gain_ref[...] * (upper + lower))
        turned = step_size / (h + 1) * jnp.concatenate([-applied[mid:], applied[:mid]], axis=0)
        if h == 0:
            out_ref[c] = state[c] + turned
            state[c] = turned
            present(1, c)
        else:
            out_ref[c] = out_ref[c] + turned

    lag = 1
    begins = {(0, 1): 0, (0, 0): lag, (1, 0): half, (1, 1): half + lag}
    present(0, 1)
    pl.semaphore_wait(barrier, 4)
    present(0, 0)
    for t in range(2 * half + lag + 1):
        live = [(h, c, t - begins[h, c]) for h, c in begins if 0 <= t - begins[h, c] <= half]
        for h, c, k in live:
            if k > 0:
                for g in range(2):
                    ag_in(h, c, g, k - 1).wait_recv()
                    if k < half:
                        ag_out(h, c, g, k).start()
        if t == 1:
            lax.fori_loop(1, n, wait_load(0), 0)
        for h, c, k in live:
            if 0 < k < half:
                for g in range(2):
                    rs_hop(h, 1 - c, g, k)
            if k == half:
                if c == 0:
                    if h == 1:
                        sym_low(0).wait_send()
                    rs_last(h, 1, low_send)
                    sym_low(h).start()
                else:
                    rs_last(h, 0, low)
        if t == 1:
            lax.fori_loop(0, n, wait_load(1), 0)
        for h, c, k in live:
            if k == 1:
                forward(h, c, me, first=True)
            if 0 < k < half:
                for g in range(2):
                    forward(h, c, at(-sign[g] * k))
            if k == half:
                forward(h, c, at(half))
                finish(h, c)
        for h, c, k in live:
            if k == 0:
                if t == 0:
                    load(0, 0).wait()
                begin(h, c)

    sym_rows(1).wait_send()
    sym_low(1).wait_send()
    for b in range(2):
        for g in range(2):
            for k in range(half):
                rs_copy(1, b, g, k).wait_send()
                for h in range(2):
                    ag_out(h, b, g, k).wait_send()


def local(coefficients, dipole, energies, pulse_field, live_states):
    n_local, n_rows, n_cols = coefficients.shape
    assert n_local == 2
    n = lax.axis_size("slab")
    n_sym_dev = lax.axis_size("sym")
    width = dipole.shape[2] // n
    first_block = lax.axis_index("sym") * n_local
    live_here = lax.dynamic_slice_in_dim(live_states, first_block, n_local)
    row_ids = lax.axis_index("slab") * n_rows + jnp.arange(n_rows, dtype=jnp.int32)
    live_mask = (row_ids[None, :] < live_here[:, None]).astype(jnp.float32)[:, None, :]
    column_gain = jnp.concatenate([pulse_field, pulse_field])[:, None]
    start_state = live_mask * jnp.transpose(coefficients, (0, 2, 1))
    half = n // 2
    hops = (2, n_local, 2, half)
    f32, bf16 = jnp.float32, jnp.bfloat16
    vmem = pl.BlockSpec(memory_space=pltpu.VMEM)
    hbm = pl.BlockSpec(memory_space=pl.ANY)
    dma = pltpu.SemaphoreType.DMA
    flops = 8 * n_local * n_rows * dipole.shape[2] * n_cols
    adjoint = pl.pallas_call(
        functools.partial(kernel, n, n_sym_dev),
        out_shape=jax.ShapeDtypeStruct((n_local, n_cols, n_rows), f32),
        in_specs=[hbm, hbm, vmem, vmem, vmem],
        out_specs=vmem,
        scratch_shapes=[
            pltpu.VMEM((n_local, n, n_rows, width), bf16),
            pltpu.VMEM((2, n_local, n, n_rows, n_cols), bf16),
            pltpu.VMEM((n_local, 2, half, n_cols, n_rows), bf16),
            pltpu.VMEM((2, n_local, 2, half, n_cols, n_rows), bf16),
            pltpu.VMEM((n_rows, n_cols), bf16),
            pltpu.VMEM((2, n_local, n_cols, n_rows), bf16),
            pltpu.VMEM((2, n_local, n_rows, n_cols), f32),
            pltpu.VMEM((n_local, n_cols, n_rows), f32),
            pltpu.VMEM((n_cols, n_rows), f32),
            pltpu.VMEM((n_cols, n_rows), f32),
            pltpu.VMEM((2, n_cols, n_rows), f32),
            dma((n_local, n)),
            dma,
            dma(hops), dma(hops), dma(hops), dma(hops),
            dma((2, 2)), dma((2, 2)),
        ],
        compiler_params=pltpu.CompilerParams(
            collective_id=0, has_side_effects=True, vmem_limit_bytes=62 * 2**20
        ),
        cost_estimate=pl.CostEstimate(flops=flops, bytes_accessed=2 * dipole.size, transcendentals=0),
    )(start_state, dipole, energies[:, None, :], live_mask, column_gain)
    return jnp.transpose(adjoint, (0, 2, 1))


def solution(mesh):
    placed = (P("sym", "slab", None), P("sym", "slab", None), P("sym", "slab"), P(), P())
    return jax.shard_map(
        local, mesh=mesh, in_specs=placed, out_specs=P("sym", "slab", None), check_vma=False
    )
```

time: 539 us -> 183 us (0.34)
  waiting for transfers between devices: 437 us -> 0 us
  Pallas kernels: 0 us -> 173 us
  matrix products: 70.8 us -> 0 us
  between operations: 13.3 us -> 0.02 us
  starting transfers between devices: 6.53 us -> 0 us
    reduce_scatter x2 -> x0, waiting for transfers between devices: 291 us -> none  [hamiltonian(): lax.psum_scatter(jnp.einsum('srk,src->ksc', row_panel, amplitude_bf, pref...]
    pallas_call x0 -> x1, Pallas kernels: none -> 173 us  [local(): pl.pallas_call(functools.partial(kernel, n, n_sym_dev), out_shape=jax.Sha...]
    all_gather x2 -> x0, waiting for transfers between devices: 142 us -> none  [hamiltonian(): lax.all_gather(upper_rows, 'slab', axis=1, tiled=True)]
    dot_general x4 -> x0, matrix products: 70.8 us -> none  [the longest x2 36.7 us: hamiltonian(): jnp.einsum('srk,src->ksc', row_panel, amplitude_bf, preferred_element_typ...]
    ppermute x4 -> x0, starting transfers between devices: 6.4 us -> none  [from_behind(): lax.ppermute(value, axis, [(source, source + steps) for source in range(i...]
  transfers between devices with their start and end apart: 8 -> 0, of which waited for: 6 -> 0; matrix products, arithmetic and copies ran while one was open for 1% -> 0% of each run, Pallas kernels for 0% -> 0%
where the time goes in v2:
time: 183 us
  Pallas kernels  173 us (95%)
  local copies, waits for them, and re-layouts  6.85 us (4%)
  other arithmetic  2.64 us (1%)
    pallas_call x1, Pallas kernels, local(): pl.pallas_call(functools.partial(kernel, n, n_sym_dev), out_shape=jax.Sha...  173 us

profile of v2, /device:TPU:0, one launch (start us, length us, event | category | flops | bytes accessed | tf_op | source)
XLA Modules:
  0.0 182.9 jit_solution(2590060460579658324)
XLA Ops:
  0.0 0.7 dynamic_slice.3
  0.7 0.8 maximum_bitcast_fusion
  1.5 0.7 compare_convert_fusion.mask_ref
  2.2 0.1 compare_convert_fusion.1
  2.3 1.3 broadcast_in_dim.4.energy_ref
  3.6 0.7 copy.7.gain_ref
  4.3 1.6 copy.6
  5.9 1.1 multiply_bitcast_fusion.start_ref
  7.0 173.4 %shard_map.55 = f32[2,128,1024]{2,1,0:T(8,128)} custom-call(f32[2,128,1024]{2,1,0:T(8,128)} %multiply_bitcast_fusion.start_ref, bf16[2,1024,8192]{2,1,0:T(8,128)(2,1)} %dip_ref.1, f32[2,1,1024]{2,1,0:T(1,128)} %broadcast_in_dim.4.energy_ref, f32[2,1,1024]{2,1,0:T(1,128)} %compare_convert_fusion.mask_ref, f32[128,1]{1,0:T(8,128)} %copy.7.gain_ref), custom_call_target="tpu_custom_call" | custom-call | flops 17179869184 | bytes 33554432 | tf_op jit(solution)/shard_map/pallas_call | solution.py:287
  180.4 2.5 %copy.8 = f32[2,1024,128]{2,1,0:T(8,128)} copy(f32[2,1024,128]{1,2,0:T(8,128)} %bitcast.5) | data formatting | bytes 2097152 | tf_op jit(solution)/shard_map/transpose | solution.py:314
  (1 shorter events, 0.0 us)

commit v3 on v2

--- a/solution.py
+++ b/solution.py
@@ -12,7 +12,7 @@
 
 
 def kernel(
-    n, n_sym_dev, start_ref, dip_ref, energy_ref, mask_ref, gain_ref, out_ref,
+    n, n_sym_dev, coef_ref, dip_ref, energy_ref, field_ref, live_ref, out_ref,
     dip, gath, rs_send, rs_recv, u_rows, u_cols, acc, state, low, low_send, low_recv,
     load_sem, start_sem, ag_send_sem, ag_recv_sem, rs_send_sem, rs_recv_sem, sym_send_sem, sym_recv_sem,
 ):
@@ -62,11 +62,17 @@
 
         return one
 
-    first_state = pltpu.make_async_copy(start_ref, state, start_sem)
+    first_state = pltpu.make_async_copy(coef_ref, acc.at[1], start_sem)
     first_state.start()
     lax.fori_loop(0, n, start_load(0), 0)
     lax.fori_loop(0, n, start_load(1), 0)
+    gain = jnp.concatenate([field_ref[...], field_ref[...]], axis=1)
+    gain = jnp.broadcast_to(gain, (cols, cols)).T[:, :1]
+    row_ids = me * rows + lax.broadcasted_iota(jnp.int32, (1, rows), 1)
+    mask = [(row_ids < live_ref[s * 2 + b]).astype(jnp.float32) for b in range(2)]
     first_state.wait()
+    for b in range(2):
+        state[b] = mask[b] * acc[1, b].T
 
     def ag_copy(h, b, g, k, owner):
         slot = gath.at[h, b, owner]
@@ -202,7 +208,7 @@
         else:
             lower = low[...]
             upper = upper * (s < n_sym_dev - 1).astype(jnp.float32)
-        applied = mask_ref[c] * (energy_ref[c] * state[c] + gain_ref[...] * (upper + lower))
+        applied = mask[c] * (energy_ref[c:c + 1] * state[c] + gain * (upper + lower))
         turned = step_size / (h + 1) * jnp.concatenate([-applied[mid:], applied[:mid]], axis=0)
         if h == 0:
             out_ref[c] = state[c] + turned
@@ -271,12 +277,6 @@
     n = lax.axis_size("slab")
     n_sym_dev = lax.axis_size("sym")
     width = dipole.shape[2] // n
-    first_block = lax.axis_index("sym") * n_local
-    live_here = lax.dynamic_slice_in_dim(live_states, first_block, n_local)
-    row_ids = lax.axis_index("slab") * n_rows + jnp.arange(n_rows, dtype=jnp.int32)
-    live_mask = (row_ids[None, :] < live_here[:, None]).astype(jnp.float32)[:, None, :]
-    column_gain = jnp.concatenate([pulse_field, pulse_field])[:, None]
-    start_state = live_mask * jnp.transpose(coefficients, (0, 2, 1))
     half = n // 2
     hops = (2, n_local, 2, half)
     f32, bf16 = jnp.float32, jnp.bfloat16
@@ -287,7 +287,7 @@
     adjoint = pl.pallas_call(
         functools.partial(kernel, n, n_sym_dev),
         out_shape=jax.ShapeDtypeStruct((n_local, n_cols, n_rows), f32),
-        in_specs=[hbm, hbm, vmem, vmem, vmem],
+        in_specs=[hbm, hbm, vmem, vmem, pl.BlockSpec(memory_space=pltpu.SMEM)],
         out_specs=vmem,
         scratch_shapes=[
             pltpu.VMEM((n_local, n, n_rows, width), bf16),
@@ -310,7 +310,7 @@
             collective_id=0, has_side_effects=True, vmem_limit_bytes=62 * 2**20
         ),
         cost_estimate=pl.CostEstimate(flops=flops, bytes_accessed=2 * dipole.size, transcendentals=0),
-    )(start_state, dipole, energies[:, None, :], live_mask, column_gain)
+    )(coefficients, dipole, energies, pulse_field[None, :], live_states)
     return jnp.transpose(adjoint, (0, 2, 1))
 
 

time: 183 us -> 177 us (0.967)
  local copies, waits for them, and re-layouts: 6.85 us -> 2.53 us
  other arithmetic: 2.64 us -> 0 us
    broadcast_in_dim x2 -> x0, local copies, waits for them, and re-layouts: 2.04 us -> none  [the longest x1 1.31 us: local(): energies[:, None, :]]
where the time goes in v3:
time: 177 us
  Pallas kernels  174 us (98%)
  local copies, waits for them, and re-layouts  2.53 us (1%)
    pallas_call x1, Pallas kernels, local(): pl.pallas_call(functools.partial(kernel, n, n_sym_dev), out_shape=jax.Sha...  174 us

profile of v3, /device:TPU:0, one launch (start us, length us, event | category | flops | bytes accessed | tf_op | source)
XLA Modules:
  0.0 176.7 jit_solution(16751552100504209868)
XLA Ops:
  0.0 174.2 %shard_map.55 = f32[2,128,1024]{2,1,0:T(8,128)} custom-call(f32[2,1024,128]{2,1,0:T(8,128)} %coef_ref.1, bf16[2,1024,8192]{2,1,0:T(8,128)(2,1)} %dip_ref.1, f32[2,1024]{1,0:T(2,128)} %energy_ref.1, f32[1,64]{1,0:T(1,128)} %bitcast.3, s32[8]{0:T(128)} %live_ref.1), custom_call_target="tpu_custom_call" | custom-call | flops 17179869184 | bytes 33554432 | tf_op jit(solution)/shard_map/pallas_call | solution.py:287
  174.2 2.5 %copy.6 = f32[2,1024,128]{2,1,0:T(8,128)} copy(f32[2,1024,128]{1,2,0:T(8,128)} %bitcast.2) | data formatting | bytes 2097152 | tf_op jit(solution)/shard_map/transpose | solution.py:314

commit v4 on v3

--- a/solution.py
+++ b/solution.py
@@ -191,7 +191,7 @@
         u_cols[h, b] = state[b].astype(jnp.bfloat16)
 
     def begin(h, c):
-        if c == 0:
+        if c == 0 and h == 1:
             for g in range(2):
                 ag_out(h, 0, g, 0).start()
         rs_first(h, 1 - c)
@@ -217,10 +217,12 @@
         else:
             out_ref[c] = out_ref[c] + turned
 
-    lag = 1
+    lag = 2
     begins = {(0, 1): 0, (0, 0): lag, (1, 0): half, (1, 1): half + lag}
     present(0, 1)
     pl.semaphore_wait(barrier, 4)
+    for g in range(2):
+        ag_out(0, 0, g, 0).start()
     present(0, 0)
     for t in range(2 * half + lag + 1):
         live = [(h, c, t - begins[h, c]) for h, c in begins if 0 <= t - begins[h, c] <= half]

time: 177 us -> 173 us (0.977)
  Pallas kernels: 174 us -> 170 us
    pallas_call x1, Pallas kernels: 174 us -> 170 us  [local(): pl.pallas_call(functools.partial(kernel, n, n_sym_dev), out_shape=jax.Sha...]
where the time goes in v4:
time: 173 us
  Pallas kernels  170 us (98%)
  local copies, waits for them, and re-layouts  2.53 us (1%)
    pallas_call x1, Pallas kernels, local(): pl.pallas_call(functools.partial(kernel, n, n_sym_dev), out_shape=jax.Sha...  170 us

profile of v4, /device:TPU:0, one launch (start us, length us, event | category | flops | bytes accessed | tf_op | source)
XLA Modules:
  0.0 172.9 jit_solution(6384022035427227119)
XLA Ops:
  0.0 170.4 %shard_map.55 = f32[2,128,1024]{2,1,0:T(8,128)} custom-call(f32[2,1024,128]{2,1,0:T(8,128)} %coef_ref.1, bf16[2,1024,8192]{2,1,0:T(8,128)(2,1)} %dip_ref.1, f32[2,1024]{1,0:T(2,128)} %energy_ref.1, f32[1,64]{1,0:T(1,128)} %bitcast.3, s32[8]{0:T(128)} %live_ref.1), custom_call_target="tpu_custom_call" | custom-call | flops 17179869184 | bytes 33554432 | tf_op jit(solution)/shard_map/pallas_call | solution.py:289
  170.4 2.5 %copy.6 = f32[2,1024,128]{2,1,0:T(8,128)} copy(f32[2,1024,128]{1,2,0:T(8,128)} %bitcast.2) | data formatting | bytes 2097152 | tf_op jit(solution)/shard_map/transpose | solution.py:316
